TPU v7x, 256 devices: a whole 4x4x8 slice. The times are simulated.
256 devices in a mesh: row: 8 (over x, core), col: 32 (over y, z).
Axes of the slice: x: 4, y: 4, z: 8, core: 2. Of those that a mesh axis runs over, the one named last changes fastest.
Arguments:
- hidden: bfloat16 [128, 8192], P('col', 'row'), may hold values from -6 to 6
- w_gate: bfloat16 [8192, 16384], P('row', 'col'), may hold values from -0.0625 to 0.0625
- w_up: bfloat16 [8192, 16384], P('row', 'col'), may hold values from -0.0625 to 0.0625
- prior: float32 [16384, 16384], P('row', 'col'), may hold values from -1 to 12, as said below
- rhs: float32 [16384, 4096], P('row', 'col'), may hold values from -6 to 6
Outputs:
- factored: float32 [16384, 16384], P('row', 'col')
- right_out: float32 [16384, 4096], P('row', 'col')
Inputs may be any that keep to these rules, and one draw needn't show every extreme that they name: prior is symmetric and positive definite, with smallest eigenvalue 0.1 or more.
All inputs are finite; a program needn't handle non-finite values.
Results may differ from a plain program's by a relative error of at most 0.0003.
Values may be sent and summed in bfloat16 or wider, within the bound.
No kernel may reach another device: no remote copies, remote signals or barrier semaphores. Data moves between devices by JAX's collectives and lax.ppermute only.
A program may use at most 64 MiB of HBM per device.

v0:
```python
import jax
import jax.numpy as jnp
from jax import lax
from jax.sharding import Mesh
from jax.sharding import PartitionSpec as P

P_SIZE = 128
PANELS = 2
COL = ("col_0", "col_1")
DAMP = 0.5


def joined_along(blocks, dim):
    blocks = jnp.moveaxis(blocks, 0, dim)
    lengths = blocks.shape
    return blocks.reshape(*lengths[:dim], lengths[dim] * lengths[dim + 1], *lengths[dim + 2 :])


def copy_for_each(shard, axis):
    peers = lax.axis_size(axis)
    return lax.all_to_all(
        jnp.broadcast_to(shard[None], (peers, *shard.shape)), axis, 0, 0, tiled=True
    )


def gathered_copies(shard, axis, dim):
    return joined_along(copy_for_each(shard, axis), dim)


def side_by_side(arrays, axis, dim, along):
    both = jnp.concatenate(arrays, axis=along)
    result, at, finished = (lax.psum_scatter(both, axis, scatter_dimension=dim, tiled=True), 0, [])
    for a in arrays:
        finished.append(lax.slice_in_dim(result, at, at + a.shape[along], axis=along))
        at += a.shape[along]
    return tuple(finished)


def spread(shard, axes, root):
    shard = jnp.where(lax.axis_index(axes) == root, shard, jnp.zeros_like(shard))
    for axis in axes:
        shard = lax.psum(shard, axis)
    return shard


def broadcast(shard, axis, root):
    return lax.dynamic_index_in_dim(lax.all_gather(shard, axis), root, 0, keepdims=False)


def local(hidden, w_gate, w_up, prior, rhs):
    rows_count = lax.axis_size("row")
    cols_count = lax.axis_size(COL)
    row_id = lax.axis_index("row")
    col_id = lax.axis_index(COL)
    ratio = cols_count // rows_count
    height, width = prior.shape
    tokens = gathered_copies(hidden, COL, 0)
    gate_part = jnp.dot(tokens, w_gate, preferred_element_type=jnp.float32)
    up_part = jnp.dot(tokens, w_up, preferred_element_type=jnp.float32)
    gate, upward = side_by_side((gate_part, up_part), "row", 0, 1)
    keys = gathered_copies(jax.nn.silu(gate) * upward, "row", 0)
    samples = keys.shape[0]
    regrouped = lax.all_to_all(keys, COL, split_axis=0, concat_axis=1, tiled=True)
    own_part = lax.dynamic_slice_in_dim(regrouped, row_id * height, height, 1)
    row_keys = gathered_copies(own_part, COL, 0)
    row_global = row_id * height + lax.iota(jnp.int32, height)
    col_global = col_id * width + lax.iota(jnp.int32, width)
    outer = lax.dot_general(
        row_keys,
        keys,
        (((0,), (0,)), ((), ())),
        precision=lax.Precision.HIGHEST,
        preferred_element_type=jnp.float32,
    )
    work = prior + outer / samples
    work = work + jnp.where(row_global[:, None] == col_global[None, :], DAMP, 0.0).astype(
        jnp.float32
    )
    right = rhs
    offsets = lax.iota(jnp.int32, P_SIZE)
    for panel in range(PANELS):
        start = panel * P_SIZE
        stop = start + P_SIZE
        column = spread(work[:, start:stop], COL, 0)
        pivot = jnp.linalg.cholesky(broadcast(column[start:stop], "row", 0))
        solved = jax.scipy.linalg.solve_triangular(pivot, column.T, lower=True).T
        placed = jnp.zeros_like(solved).at[start:stop].set(pivot)
        in_pivot = (row_global >= start) & (row_global < stop)
        beyond = row_global >= stop
        factor_cols = jnp.where(in_pivot[:, None], placed, jnp.where(beyond[:, None], solved, 0.0))
        matching = lax.dynamic_slice_in_dim(factor_cols, col_id % ratio * width, width, 0)
        across = broadcast(matching, "row", col_id // ratio)
        lower_rows = jnp.where(beyond[:, None], factor_cols, 0.0)
        upper_cols = jnp.where((col_global >= stop)[:, None], across, 0.0)
        work = work - lax.dot_general(
            lower_rows,
            upper_cols,
            (((1,), (1,)), ((), ())),
            precision=lax.Precision.HIGHEST,
            preferred_element_type=jnp.float32,
        )
        solution = jax.scipy.linalg.solve_triangular(
            factor_cols[start:stop], right[start:stop], lower=True
        )
        solution = broadcast(solution, "row", 0)
        right = right - jnp.dot(
            lower_rows,
            solution,
            precision=lax.Precision.HIGHEST,
            preferred_element_type=jnp.float32,
        )
        right = right.at[start:stop].set(jnp.where(row_id == 0, solution, right[start:stop]))
        keep_factor = (row_global[:, None] >= start + offsets[None, :]) & (col_id == 0)
        work = work.at[:, start:stop].set(jnp.where(keep_factor, factor_cols, work[:, start:stop]))
    return (work, right)


def solution(mesh):
    finer = Mesh(mesh.devices.reshape(mesh.shape["row"], 4, 8), ("row", "col_0", "col_1"))
    placed = (P(COL, "row"), P("row", COL), P("row", COL), P("row", COL), P("row", COL))
    return jax.shard_map(
        local,
        mesh=finer,
        in_specs=placed,
        out_specs=(P("row", COL), P("row", COL)),
        check_vma=False,
    )
```

profile of v0, /device:TPU:1, one launch (start us, length us, event | category | flops | bytes accessed | tf_op | source)
XLA Modules:
  0.0 588.0 jit_solution(16554936312668972503)
XLA Ops:
  8.1 21.5 %all_to_all.34 = bf16[32,4,1024]{2,1,0:T(4,128)(2,1)S(1)} all-to-all(bf16[32,4,1024]{2,1,0:T(4,128)(2,1)S(1)} %broadcast_in_dim.100), channel_id=1, replica_groups=mesh['row'=8,'col_0'=4,'col_1'=8] {'col_0','col_1'}, dimensions={0} | all-to-all | bytes 524288 | tf_op jit(solution)/shard_map/all_to_all | solution.py:21
  32.4 30.2 %reduce-scatter.2.cloned.1.call-done = f32[16,1024]{1,0:T(8,128)} async-done(((f32[128,1024]{1,0:T(8,128)}), f32[16,1024]{1,0:T(8,128)}) %reduce-scatter.2.cloned.1.call-update) | async-done | bytes 65552 | tf_op jit(solution)/shard_map/reduce_scatter | solution.py:32
  63.4 11.9 %all_to_all.35 = f32[8,16,512]{2,1,0:T(8,128)S(1)} all-to-all(f32[8,16,512]{2,1,0:T(8,128)S(1)} %broadcast_in_dim.101), channel_id=1, replica_groups=mesh['row'=8,'col_0'=4,'col_1'=8] {'row'}, dimensions={0} | all-to-all | bytes 524288 | tf_op jit(solution)/shard_map/all_to_all | solution.py:21
  76.0 9.6 %all-to-all-start.2 = ((f32[32,4,512]{2,1,0:T(4,128)}), f32[32,4,512]{2,1,0:T(4,128)S(1)}, u32[]{:S(2)}, u32[]{:S(2)}) async-start(f32[32,4,512]{2,1,0:T(4,128)} %all_to_all.25), calls=%async_computation.3 | async-start | bytes 524288 | tf_op jit(solution)/shard_map/all_to_all | solution.py:63
  85.6 9.7 %all-to-all-done.2 = f32[32,4,512]{2,1,0:T(4,128)S(1)} async-done(((f32[32,4,512]{2,1,0:T(4,128)}), f32[32,4,512]{2,1,0:T(4,128)S(1)}, u32[]{:S(2)}, u32[]{:S(2)}) %all-to-all-start.2) | async-done | bytes 262176 | tf_op jit(solution)/shard_map/all_to_all | solution.py:63
  96.5 6.0 %all-to-all-start.3 = ((f32[32,4,2048]{2,1,0:T(4,128)}), f32[32,4,2048]{2,1,0:T(4,128)S(1)}, u32[]{:S(2)}, u32[]{:S(2)}) async-start(f32[32,4,2048]{2,1,0:T(4,128)} %broadcast_in_dim.102), calls=%async_computation.4 | async-start | bytes 2097152 | tf_op jit(solution)/shard_map/all_to_all | solution.py:21
  102.6 24.3 %all-to-all-done.3 = f32[32,4,2048]{2,1,0:T(4,128)S(1)} async-done(((f32[32,4,2048]{2,1,0:T(4,128)}), f32[32,4,2048]{2,1,0:T(4,128)S(1)}, u32[]{:S(2)}, u32[]{:S(2)}) %all-to-all-start.3) | async-done | bytes 1048608 | tf_op jit(solution)/shard_map/all_to_all | solution.py:21
  127.3 5.8 select_add_fusion
  133.1 2.0 copy-done.2
  136.3 48.9 %all-reduce.7.cloned.1.call-done = f32[2048,128]{1,0:T(8,128)} async-done(((f32[2048,128]{1,0:T(8,128)}), f32[2048,128]{1,0:T(8,128)}) %all-reduce.7.cloned.1.call-update) | async-done | bytes 1048592 | tf_op jit(solution)/shard_map/psum | solution.py:42
  185.3 76.3 %all-reduce.9.cloned.1.call-done = f32[2048,128]{1,0:T(8,128)} async-done(((f32[2048,128]{1,0:T(8,128)}), f32[2048,128]{1,0:T(8,128)}) %all-reduce.9.cloned.1.call-update) | async-done | bytes 1048592 | tf_op jit(solution)/shard_map/psum | solution.py:42
  262.5 18.2 %all-gather = f32[1024,128]{1,0:T(8,128)S(1)} all-gather(f32[128,128]{1,0:T(8,128)S(1)} %slice.179), channel_id=2, replica_groups=mesh['row'=8,'col_0'=4,'col_1'=8] {'row'}, dimensions={0}, use_global_device_ids=true | all-gather | bytes 589824 | tf_op jit(solution)/shard_map/all_gather | solution.py:47
  280.9 11.7 %cholesky.44 = f32[128,128]{1,0:T(8,128)S(1)} custom-call(f32[128,128]{1,0:T(8,128)S(1)} %copy.8), custom_call_target="Cholesky" | custom-call | tf_op jit(solution)/shard_map/jit(cholesky)/cholesky | solution.py:85
  294.0 9.8 %custom-call.10 = f32[1,128,128]{1,2,0:T(8,128)S(1)} custom-call(f32[1,128,128]{2,1,0:T(8,128)S(1)} %get-tuple-element.79), custom_call_target="InvertDiagBlocksLowerTriangular" | custom-call | tf_op jit(solution)/shard_map/jit(_solve_triangular)/triangular_solve | solution.py:86
  303.8 3.3 fusion.3
  308.5 24.7 %all-gather.9.cloned.1.call-done = f32[4096,128]{1,0:T(8,128)} async-done(((f32[512,128]{1,0:T(8,128)}), f32[4096,128]{1,0:T(8,128)}) %all-gather.9.cloned.1.call-update) | async-done | bytes 2097168 | tf_op jit(solution)/shard_map/all_gather | solution.py:47
  333.3 5.5 convolution_subtract_fusion.1
  339.9 2.0 copy-done.1
  343.1 49.5 %all-reduce.11.cloned.1.call-done = f32[2048,128]{1,0:T(8,128)} async-done(((f32[2048,128]{1,0:T(8,128)}), f32[2048,128]{1,0:T(8,128)}) %all-reduce.11.cloned.1.call-update) | async-done | bytes 1048592 | tf_op jit(solution)/shard_map/psum | solution.py:42
  392.7 76.3 %all-reduce.13.cloned.1.call-done = f32[2048,128]{1,0:T(8,128)} async-done(((f32[2048,128]{1,0:T(8,128)}), f32[2048,128]{1,0:T(8,128)}) %all-reduce.13.cloned.1.call-update) | async-done | bytes 1048592 | tf_op jit(solution)/shard_map/psum | solution.py:42
  469.9 18.3 %all-gather.2 = f32[1024,128]{1,0:T(8,128)S(1)} all-gather(f32[128,128]{1,0:T(8,128)S(1)} %slice.183), channel_id=4, replica_groups=mesh['row'=8,'col_0'=4,'col_1'=8] {'row'}, dimensions={0}, use_global_device_ids=true | all-gather | bytes 589824 | tf_op jit(solution)/shard_map/all_gather | solution.py:47
  488.3 11.7 %cholesky.55 = f32[128,128]{1,0:T(8,128)S(1)} custom-call(f32[128,128]{1,0:T(8,128)S(1)} %copy.11), custom_call_target="Cholesky" | custom-call | tf_op jit(solution)/shard_map/jit(cholesky)/cholesky | solution.py:85
  501.4 9.8 %custom-call.11 = f32[1,128,128]{1,2,0:T(8,128)S(1)} custom-call(f32[1,128,128]{2,1,0:T(8,128)S(1)} %get-tuple-element.77), custom_call_target="InvertDiagBlocksLowerTriangular" | custom-call | tf_op jit(solution)/shard_map/jit(_solve_triangular)/triangular_solve | solution.py:86
  511.2 3.2 fusion.1
  515.9 9.8 %custom-call.12 = f32[1,128,128]{1,2,0:T(8,128)S(1)} custom-call(f32[1,128,128]{2,1,0:T(8,128)S(1)} %fusion.32), custom_call_target="InvertDiagBlocksLowerTriangular" | custom-call | tf_op jit(solution)/shard_map/jit(_solve_triangular)/triangular_solve | solution.py:102
  526.9 14.2 %all-gather.4 = f32[1024,128]{1,0:T(8,128)S(1)} all-gather(f32[128,128]{1,0:T(8,128)S(1)} %fusion.34), channel_id=6, replica_groups=mesh['row'=8,'col_0'=4,'col_1'=8] {'row'}, dimensions={0}, use_global_device_ids=true | all-gather | bytes 589824 | tf_op jit(solution)/shard_map/all_gather | solution.py:47
  541.1 3.1 convolution_subtract_fusion.3
  545.7 9.8 %custom-call.13 = f32[1,128,128]{1,2,0:T(8,128)S(1)} custom-call(f32[1,128,128]{2,1,0:T(8,128)S(1)} %fusion.30), custom_call_target="InvertDiagBlocksLowerTriangular" | custom-call | tf_op jit(solution)/shard_map/jit(_solve_triangular)/triangular_solve | solution.py:102
  556.6 13.1 %all-gather.5 = f32[1024,128]{1,0:T(8,128)S(1)} all-gather(f32[128,128]{1,0:T(8,128)S(1)} %fusion.28), channel_id=7, replica_groups=mesh['row'=8,'col_0'=4,'col_1'=8] {'row'}, dimensions={0}, use_global_device_ids=true | all-gather | bytes 589824 | tf_op jit(solution)/shard_map/all_gather | solution.py:47
  569.8 2.3 convolution_subtract_fusion.2
  572.1 5.9 %convolution_subtract_fusion = f32[2048,512]{1,0:T(8,128)S(1)} fusion(f32[2048,512]{1,0:T(8,128)} %copy-done.1, f32[2048,128]{1,0:T(8,128)S(1)} %fusion.1, pred[2048]{0:T(1024)(128)(4,1)S(1)} %fusion.44, f32[8,512,128]{2,1,0:T(8,128)} %bitcast.62, s32[]{:T(128)S(6)} %select_n.113, pred[512]{0:T(512)(128)(4,1)S(1)} %fusion.52), kind=kOutput, calls=%fused_computation.1 | convolution fusion | flops 1611988992 | bytes 9701892 | tf_op jit(solution)/shard_map/dot_general | solution.py:95
  579.1 2.0 copy-done.3
  (71 shorter events, 22.9 us)
Async XLA Ops:
  7.2 22.5 %copy-start = (bf16[1024,512]{1,0:T(8,128)(2,1)S(1)}, bf16[1024,512]{1,0:T(8,128)(2,1)}, u32[]{:S(2)}) copy-start(bf16[1024,512]{1,0:T(8,128)(2,1)} %param.23) | copy-start | bytes 3145732
  7.2 55.4 %reduce-scatter.2.cloned.1.call-start = ((), (), s32[]{:S(2)}) async-start(), calls=%async_computation.5 | async-start | bytes 589824 | tf_op jit(solution)/shard_map/reduce_scatter | solution.py:32
  76.0 19.2 %all-to-all-start.2 = ((f32[32,4,512]{2,1,0:T(4,128)}), f32[32,4,512]{2,1,0:T(4,128)S(1)}, u32[]{:S(2)}, u32[]{:S(2)}) async-start(f32[32,4,512]{2,1,0:T(4,128)} %all_to_all.25), calls=%async_computation.3 | async-start | bytes 524288 | tf_op jit(solution)/shard_map/all_to_all | solution.py:63
  96.5 30.5 %all-to-all-start.3 = ((f32[32,4,2048]{2,1,0:T(4,128)}), f32[32,4,2048]{2,1,0:T(4,128)S(1)}, u32[]{:S(2)}, u32[]{:S(2)}) async-start(f32[32,4,2048]{2,1,0:T(4,128)} %broadcast_in_dim.102), calls=%async_computation.4 | async-start | bytes 2097152 | tf_op jit(solution)/shard_map/all_to_all | solution.py:21
  102.6 82.6 %all-reduce.7.cloned.1.call-start = ((), (), s32[]{:S(2)}) async-start(), calls=%async_computation.6 | async-start | bytes 2097152 | tf_op jit(solution)/shard_map/psum | solution.py:42
  133.1 2.0 copy-start.2
  136.3 125.4 %all-reduce.9.cloned.1.call-start = ((), (), s32[]{:S(2)}) async-start(), calls=%async_computation.7 | async-start | bytes 2097152 | tf_op jit(solution)/shard_map/psum | solution.py:42
  185.2 148.1 %all-gather.9.cloned.1.call-start = ((), (), s32[]{:S(2)}) async-start(), calls=%async_computation.10 | async-start | bytes 2359296 | tf_op jit(solution)/shard_map/all_gather | solution.py:47
  307.8 84.8 %all-reduce.11.cloned.1.call-start = ((), (), s32[]{:S(2)}) async-start(), calls=%async_computation.8 | async-start | bytes 2097152 | tf_op jit(solution)/shard_map/psum | solution.py:42
  339.9 2.0 copy-start.1
  343.0 126.0 %all-reduce.13.cloned.1.call-start = ((), (), s32[]{:S(2)}) async-start(), calls=%async_computation.9 | async-start | bytes 2097152 | tf_op jit(solution)/shard_map/psum | solution.py:42
  392.6 179.5 %all-gather.11.cloned.1.call-start = ((), (), s32[]{:S(2)}) async-start(), calls=%async_computation.11 | async-start | bytes 2359296 | tf_op jit(solution)/shard_map/all_gather | solution.py:47
  572.1 5.9 %copy-start.4 = (f32[2048,128]{1,0:T(8,128)}, f32[2048,128]{1,0:T(8,128)S(1)}, u32[]{:S(2)}) copy-start(f32[2048,128]{1,0:T(8,128)S(1)} %fusion.27) | copy-start | bytes 3145732
  579.1 2.0 copy-start.3
Sparse Core Ops, SparseCore 0:
  32.5 29.9 reduce-scatter.1
  136.4 48.7 all-reduce.6
  187.5 74.0 all-reduce.8
  307.9 25.3 all-gather.8
  343.1 49.4 all-reduce.10
  394.9 74.0 all-reduce.12
  515.4 26.1 all-gather.10
where the time goes:
time: 589 us; the launch traced here: 588 us
  waiting for transfers between devices  340 us (58%)
  blocking collectives  97.3 us (17%)
  other arithmetic  74.2 us (13%)
  matrix products  33.2 us (6%)
  starting transfers between devices  15.9 us (3%)
  between operations  14.5 us (2%)
  local copies, waits for them, and re-layouts  12.9 us (2%)
    psum x4, waiting for transfers between devices, spread(): shard = lax.psum(shard, axis)  251 us
    all_gather x4, blocking collectives, broadcast(): lax.all_gather(shard, axis)  63.8 us
    all_to_all x2, blocking collectives, copy_for_each(): lax.all_to_all(jnp.broadcast_to(shard[None], (peers, *shard.shape)), axis...  33.4 us
    reduce_scatter x1, waiting for transfers between devices, side_by_side(): lax.psum_scatter(both, axis, scatter_dimension=dim, tiled=True)  30.2 us
    another operation x6, other arithmetic, local(): pivot = jnp.linalg.cholesky(broadcast(column[start:stop], 'row', 0))  24.8 us
    all_gather x2, waiting for transfers between devices, broadcast(): lax.all_gather(shard, axis)  24.7 us
    all_to_all x1, waiting for transfers between devices, copy_for_each(): lax.all_to_all(jnp.broadcast_to(shard[None], (peers, *shard.shape)), axis...  24.3 us
    another operation x4, other arithmetic, local(): solved = jax.scipy.linalg.solve_triangular(pivot, column.T, lower=True).T  20.9 us
  transfers between devices with their start and end apart: 9, of which 8 were waited for; matrix products, arithmetic and copies ran while one was open for 5% of the time, Pallas kernels for 0%

commit v1 on v0

--- a/solution.py
+++ b/solution.py
@@ -60,7 +60,9 @@
     gate, upward = side_by_side((gate_part, up_part), "row", 0, 1)
     keys = gathered_copies(jax.nn.silu(gate) * upward, "row", 0)
     samples = keys.shape[0]
-    regrouped = lax.all_to_all(keys, COL, split_axis=0, concat_axis=1, tiled=True)
+    regrouped = jnp.concatenate(
+        lax.all_to_all(jnp.stack(jnp.split(keys, lax.axis_size(COL), axis=0)), COL, 0, 0), axis=1
+    )
     own_part = lax.dynamic_slice_in_dim(regrouped, row_id * height, height, 1)
     row_keys = gathered_copies(own_part, COL, 0)
     row_global = row_id * height + lax.iota(jnp.int32, height)

time: 589 us -> 607 us (1.031)
  local copies, waits for them, and re-layouts: 12.9 us -> 31.3 us
    unnamed x10 -> x41, local copies, waits for them, and re-layouts: 6.04 us -> 24.6 us
where the time goes in v1:
time: 607 us
  waiting for transfers between devices  340 us (56%)
  blocking collectives  97.3 us (16%)
  other arithmetic  74.2 us (12%)
  matrix products  33.2 us (5%)
  local copies, waits for them, and re-layouts  31.3 us (5%)
  starting transfers between devices  15.9 us (3%)
  between operations  14.6 us (2%)
    psum x4, waiting for transfers between devices, spread(): shard = lax.psum(shard, axis)  251 us
    all_gather x4, blocking collectives, broadcast(): lax.all_gather(shard, axis)  63.9 us
    all_to_all x2, blocking collectives, copy_for_each(): lax.all_to_all(jnp.broadcast_to(shard[None], (peers, *shard.shape)), axis...  33.4 us
    reduce_scatter x1, waiting for transfers between devices, side_by_side(): lax.psum_scatter(both, axis, scatter_dimension=dim, tiled=True)  30.2 us
    another operation x6, other arithmetic, local(): pivot = jnp.linalg.cholesky(broadcast(column[start:stop], 'row', 0))  24.8 us
    all_gather x2, waiting for transfers between devices, broadcast(): lax.all_gather(shard, axis)  24.7 us
    unnamed x41, local copies, waits for them, and re-layouts  24.6 us
    all_to_all x1, waiting for transfers between devices, copy_for_each(): lax.all_to_all(jnp.broadcast_to(shard[None], (peers, *shard.shape)), axis...  24.3 us
  transfers between devices with their start and end apart: 9, of which 8 were waited for; matrix products, arithmetic and copies ran while one was open for 5% of the time, Pallas kernels for 0%

profile of v1, /device:TPU:1, one launch (start us, length us, event | category | flops | bytes accessed | tf_op | source)
XLA Modules:
  0.0 606.5 jit_solution(6132937201507431681)
XLA Ops:
  8.1 21.5 %all_to_all.20 = bf16[32,4,1024]{2,1,0:T(4,128)(2,1)S(1)} all-to-all(bf16[32,4,1024]{2,1,0:T(4,128)(2,1)S(1)} %broadcast_in_dim.100), channel_id=1, replica_groups=mesh['row'=8,'col_0'=4,'col_1'=8] {'col_0','col_1'}, dimensions={0} | all-to-all | bytes 524288 | tf_op jit(solution)/shard_map/all_to_all | solution.py:21
  32.4 30.2 %reduce-scatter.2.cloned.1.call-done = f32[16,1024]{1,0:T(8,128)} async-done(((f32[128,1024]{1,0:T(8,128)}), f32[16,1024]{1,0:T(8,128)}) %reduce-scatter.2.cloned.1.call-update) | async-done | bytes 65552 | tf_op jit(solution)/shard_map/reduce_scatter | solution.py:32
  63.4 11.9 %all_to_all.21 = f32[8,16,512]{2,1,0:T(8,128)S(1)} all-to-all(f32[8,16,512]{2,1,0:T(8,128)S(1)} %broadcast_in_dim.101), channel_id=1, replica_groups=mesh['row'=8,'col_0'=4,'col_1'=8] {'row'}, dimensions={0} | all-to-all | bytes 524288 | tf_op jit(solution)/shard_map/all_to_all | solution.py:21
  94.5 9.6 %all-to-all-start.2 = ((f32[32,4,512]{2,1,0:T(4,128)}), f32[32,4,512]{2,1,0:T(4,128)S(1)}, u32[]{:S(2)}, u32[]{:S(2)}) async-start(f32[32,4,512]{2,1,0:T(4,128)} %constant_dynamic-update-slice_fusion), calls=%async_computation.3 | async-start | bytes 524288 | tf_op jit(solution)/shard_map/all_to_all | solution.py:64
  104.1 9.7 %all-to-all-done.2 = f32[32,4,512]{2,1,0:T(4,128)S(1)} async-done(((f32[32,4,512]{2,1,0:T(4,128)}), f32[32,4,512]{2,1,0:T(4,128)S(1)}, u32[]{:S(2)}, u32[]{:S(2)}) %all-to-all-start.2) | async-done | bytes 262176 | tf_op jit(solution)/shard_map/all_to_all | solution.py:64
  115.0 6.0 all-to-all-start.3
  121.1 24.3 %all-to-all-done.3 = f32[32,4,2048]{2,1,0:T(4,128)S(1)} async-done(((f32[32,4,2048]{2,1,0:T(4,128)}), f32[32,4,2048]{2,1,0:T(4,128)S(1)}, u32[]{:S(2)}, u32[]{:S(2)}) %all-to-all-start.3) | async-done | bytes 1048608 | tf_op jit(solution)/shard_map/all_to_all | solution.py:21
  145.8 5.8 select_add_fusion
  151.6 2.0 copy-done.2
  154.8 48.9 %all-reduce.7.cloned.1.call-done = f32[2048,128]{1,0:T(8,128)} async-done(((f32[2048,128]{1,0:T(8,128)}), f32[2048,128]{1,0:T(8,128)}) %all-reduce.7.cloned.1.call-update) | async-done | bytes 1048592 | tf_op jit(solution)/shard_map/psum | solution.py:42
  203.7 76.3 %all-reduce.9.cloned.1.call-done = f32[2048,128]{1,0:T(8,128)} async-done(((f32[2048,128]{1,0:T(8,128)}), f32[2048,128]{1,0:T(8,128)}) %all-reduce.9.cloned.1.call-update) | async-done | bytes 1048592 | tf_op jit(solution)/shard_map/psum | solution.py:42
  280.9 18.2 %all-gather = f32[1024,128]{1,0:T(8,128)S(1)} all-gather(f32[128,128]{1,0:T(8,128)S(1)} %slice.179), channel_id=2, replica_groups=mesh['row'=8,'col_0'=4,'col_1'=8] {'row'}, dimensions={0}, use_global_device_ids=true | all-gather | bytes 589824 | tf_op jit(solution)/shard_map/all_gather | solution.py:47
  299.4 11.7 %cholesky.44 = f32[128,128]{1,0:T(8,128)S(1)} custom-call(f32[128,128]{1,0:T(8,128)S(1)} %copy.8), custom_call_target="Cholesky" | custom-call | tf_op jit(solution)/shard_map/jit(cholesky)/cholesky | solution.py:87
  312.4 9.8 %custom-call.10 = f32[1,128,128]{1,2,0:T(8,128)S(1)} custom-call(f32[1,128,128]{2,1,0:T(8,128)S(1)} %get-tuple-element.79), custom_call_target="InvertDiagBlocksLowerTriangular" | custom-call | tf_op jit(solution)/shard_map/jit(_solve_triangular)/triangular_solve | solution.py:88
  322.2 3.3 fusion.3
  327.0 24.7 %all-gather.9.cloned.1.call-done = f32[4096,128]{1,0:T(8,128)} async-done(((f32[512,128]{1,0:T(8,128)}), f32[4096,128]{1,0:T(8,128)}) %all-gather.9.cloned.1.call-update) | async-done | bytes 2097168 | tf_op jit(solution)/shard_map/all_gather | solution.py:47
  351.7 5.5 convolution_subtract_fusion.1
  358.3 2.0 copy-done.1
  361.5 49.6 %all-reduce.11.cloned.1.call-done = f32[2048,128]{1,0:T(8,128)} async-done(((f32[2048,128]{1,0:T(8,128)}), f32[2048,128]{1,0:T(8,128)}) %all-reduce.11.cloned.1.call-update) | async-done | bytes 1048592 | tf_op jit(solution)/shard_map/psum | solution.py:42
  411.2 76.3 %all-reduce.13.cloned.1.call-done = f32[2048,128]{1,0:T(8,128)} async-done(((f32[2048,128]{1,0:T(8,128)}), f32[2048,128]{1,0:T(8,128)}) %all-reduce.13.cloned.1.call-update) | async-done | bytes 1048592 | tf_op jit(solution)/shard_map/psum | solution.py:42
  488.4 18.3 %all-gather.2 = f32[1024,128]{1,0:T(8,128)S(1)} all-gather(f32[128,128]{1,0:T(8,128)S(1)} %slice.183), channel_id=4, replica_groups=mesh['row'=8,'col_0'=4,'col_1'=8] {'row'}, dimensions={0}, use_global_device_ids=true | all-gather | bytes 589824 | tf_op jit(solution)/shard_map/all_gather | solution.py:47
  506.8 11.7 %cholesky.55 = f32[128,128]{1,0:T(8,128)S(1)} custom-call(f32[128,128]{1,0:T(8,128)S(1)} %copy.11), custom_call_target="Cholesky" | custom-call | tf_op jit(solution)/shard_map/jit(cholesky)/cholesky | solution.py:87
  519.9 9.8 %custom-call.11 = f32[1,128,128]{1,2,0:T(8,128)S(1)} custom-call(f32[1,128,128]{2,1,0:T(8,128)S(1)} %get-tuple-element.77), custom_call_target="InvertDiagBlocksLowerTriangular" | custom-call | tf_op jit(solution)/shard_map/jit(_solve_triangular)/triangular_solve | solution.py:88
  529.7 3.2 fusion.1
  534.4 9.8 %custom-call.12 = f32[1,128,128]{1,2,0:T(8,128)S(1)} custom-call(f32[1,128,128]{2,1,0:T(8,128)S(1)} %fusion.32), custom_call_target="InvertDiagBlocksLowerTriangular" | custom-call | tf_op jit(solution)/shard_map/jit(_solve_triangular)/triangular_solve | solution.py:104
  545.4 14.2 %all-gather.4 = f32[1024,128]{1,0:T(8,128)S(1)} all-gather(f32[128,128]{1,0:T(8,128)S(1)} %fusion.34), channel_id=6, replica_groups=mesh['row'=8,'col_0'=4,'col_1'=8] {'row'}, dimensions={0}, use_global_device_ids=true | all-gather | bytes 589824 | tf_op jit(solution)/shard_map/all_gather | solution.py:47
  559.6 3.1 convolution_subtract_fusion.3
  564.2 9.8 %custom-call.13 = f32[1,128,128]{1,2,0:T(8,128)S(1)} custom-call(f32[1,128,128]{2,1,0:T(8,128)S(1)} %fusion.30), custom_call_target="InvertDiagBlocksLowerTriangular" | custom-call | tf_op jit(solution)/shard_map/jit(_solve_triangular)/triangular_solve | solution.py:104
  575.1 13.1 %all-gather.5 = f32[1024,128]{1,0:T(8,128)S(1)} all-gather(f32[128,128]{1,0:T(8,128)S(1)} %fusion.28), channel_id=7, replica_groups=mesh['row'=8,'col_0'=4,'col_1'=8] {'row'}, dimensions={0}, use_global_device_ids=true | all-gather | bytes 589824 | tf_op jit(solution)/shard_map/all_gather | solution.py:47
  588.3 2.3 convolution_subtract_fusion.2
  590.7 5.9 convolution_subtract_fusion
  597.7 2.0 copy-done.3
  (102 shorter events, 41.3 us)
Async XLA Ops:
  7.2 22.5 %copy-start = (bf16[1024,512]{1,0:T(8,128)(2,1)S(1)}, bf16[1024,512]{1,0:T(8,128)(2,1)}, u32[]{:S(2)}) copy-start(bf16[1024,512]{1,0:T(8,128)(2,1)} %param.23) | copy-start | bytes 3145732
  7.2 55.4 %reduce-scatter.2.cloned.1.call-start = ((), (), s32[]{:S(2)}) async-start(), calls=%async_computation.5 | async-start | bytes 589824 | tf_op jit(solution)/shard_map/reduce_scatter | solution.py:32
  94.5 19.2 %all-to-all-start.2 = ((f32[32,4,512]{2,1,0:T(4,128)}), f32[32,4,512]{2,1,0:T(4,128)S(1)}, u32[]{:S(2)}, u32[]{:S(2)}) async-start(f32[32,4,512]{2,1,0:T(4,128)} %constant_dynamic-update-slice_fusion), calls=%async_computation.3 | async-start | bytes 524288 | tf_op jit(solution)/shard_map/all_to_all | solution.py:64
  115.0 30.5 %all-to-all-start.3 = ((f32[32,4,2048]{2,1,0:T(4,128)}), f32[32,4,2048]{2,1,0:T(4,128)S(1)}, u32[]{:S(2)}, u32[]{:S(2)}) async-start(f32[32,4,2048]{2,1,0:T(4,128)} %broadcast_in_dim.102), calls=%async_computation.4 | async-start | bytes 2097152 | tf_op jit(solution)/shard_map/all_to_all | solution.py:21
  121.0 82.6 %all-reduce.7.cloned.1.call-start = ((), (), s32[]{:S(2)}) async-start(), calls=%async_computation.6 | async-start | bytes 2097152 | tf_op jit(solution)/shard_map/psum | solution.py:42
  151.6 2.0 copy-start.2
  154.7 125.4 %all-reduce.9.cloned.1.call-start = ((), (), s32[]{:S(2)}) async-start(), calls=%async_computation.7 | async-start | bytes 2097152 | tf_op jit(solution)/shard_map/psum | solution.py:42
  203.7 148.1 %all-gather.9.cloned.1.call-start = ((), (), s32[]{:S(2)}) async-start(), calls=%async_computation.10 | async-start | bytes 2359296 | tf_op jit(solution)/shard_map/all_gather | solution.py:47
  326.3 84.9 %all-reduce.11.cloned.1.call-start = ((), (), s32[]{:S(2)}) async-start(), calls=%async_computation.8 | async-start | bytes 2097152 | tf_op jit(solution)/shard_map/psum | solution.py:42
  358.3 2.0 copy-start.1
  361.5 126.1 %all-reduce.13.cloned.1.call-start = ((), (), s32[]{:S(2)}) async-start(), calls=%async_computation.9 | async-start | bytes 2097152 | tf_op jit(solution)/shard_map/psum | solution.py:42
  411.1 179.5 %all-gather.11.cloned.1.call-start = ((), (), s32[]{:S(2)}) async-start(), calls=%async_computation.11 | async-start | bytes 2359296 | tf_op jit(solution)/shard_map/all_gather | solution.py:47
  590.6 5.9 copy-start.4
  597.6 2.0 copy-start.3
Sparse Core Ops, SparseCore 0:
  32.5 29.9 reduce-scatter.1
  154.8 48.7 all-reduce.6
  206.0 74.0 all-reduce.8
  326.4 25.3 all-gather.8
  361.6 49.4 all-reduce.10
  413.4 74.0 all-reduce.12
  533.9 26.1 all-gather.10
